TPU v7x, 32 devices: a whole 2x2x4 slice. The times are simulated.
32 devices in a mesh: dp: 8 (over z, y), mp: 4 (over x, core).
Axes of the slice: x: 2, y: 2, z: 4, core: 2. Of those that a mesh axis runs over, the one named last changes fastest.
Arguments:
- tokens: bfloat16 [8192, 2048], P('dp'), may hold values from -6 to 6
- documents: int32 [8, 1024], P('dp'), may hold values from 0 to 3, never falling along the last dimension, each value on 1 to 512 neighbouring positions
- cotangent: bfloat16 [8192, 2048], P('dp'), may hold values from -6 to 6
- attn_gain: float32 [2048], P('dp'), may hold values from 0.5 to 1.5
- query_gain: float32 [128], P('dp'), may hold values from 1 to 2
- key_norm_scale: float32 [128], P('dp'), may hold values from 0.25 to 1.75
- query_weight: float32 [2048, 2048], P('dp', 'mp'), may hold values from -0.125 to 0.125
- key_projection: float32 [2048, 1024], P('dp', 'mp'), may hold values from -0.125 to 0.125
- value_projection: float32 [2048, 1024], P('dp', 'mp'), may hold values from -0.125 to 0.125
- output_weight: float32 [2048, 2048], P('mp', 'dp'), may hold values from -1 to 1
- mlp_gain: float32 [2048], P('dp'), may hold values from 0.5 to 1.5
- gate_weight: float32 [2048, 6144], P('dp', 'mp'), may hold values from -0.125 to 0.125
- up_weight: float32 [2048, 6144], P('dp', 'mp'), may hold values from -0.125 to 0.125
- down_weight: float32 [6144, 2048], P('mp', 'dp'), may hold values from -0.078125 to 0.078125
Outputs:
- layer_output: bfloat16 [8192, 2048], P(('dp', 'mp'))
- input_grad: float32 [8192, 2048], P(('dp', 'mp'))
- attn_gain_grad: float32 [2048], P('dp')
- query_gain_grad: float32 [128], P('dp')
- key_gain_grad: float32 [128], P('dp')
- query_weight_grad: float32 [2048, 2048], P('dp', 'mp')
- key_weight_grad: float32 [2048, 1024], P('dp', 'mp')
- value_weight_grad: float32 [2048, 1024], P('dp', 'mp')
- output_weight_grad: float32 [2048, 2048], P('mp', 'dp')
- mlp_gain_grad: float32 [2048], P('dp')
- gate_weight_grad: float32 [2048, 6144], P('dp', 'mp')
- up_weight_grad: float32 [2048, 6144], P('dp', 'mp')
- down_weight_grad: float32 [6144, 2048], P('mp', 'dp')
Inputs may be any that keep to these rules, and one draw needn't show every extreme that they name: `documents`: document numbers never fall along a sequence; each document holds 1 to 512 positions, and some document holds exactly 512.
All inputs are finite; a program needn't handle non-finite values.
Results may differ from a plain program's by a relative error of at most 0.023.
Values may be sent and summed in bfloat16 or wider, within the bound.
A program may use at most 256 MiB of HBM per device.

v0:
```python
import jax
import jax.numpy as jnp
from jax import lax
from jax.sharding import PartitionSpec as P

QUERY_HEADS = 16
KEY_VALUE_HEADS = 8
HEAD_WIDTH = 128
EPSILON = 1e-06
MASKED = -1e30


def doc_positions(documents):
    indices = jnp.arange(documents.shape[-1], dtype=jnp.int32)
    boundary = jnp.concatenate(
        [
            jnp.ones(documents.shape[:-1] + (1,), dtype=jnp.bool_),
            documents[:, 1:] != documents[:, :-1],
        ],
        -1,
    )
    starts = lax.cummax(jnp.where(boundary, indices[None, :], 0), axis=1)
    return indices[None, :] - starts


def rope_tables(positions, head_size):
    middle = head_size // 2
    frequency = jnp.power(1000000.0, -2.0 * jnp.arange(middle, dtype=jnp.float32) / head_size)
    angles = positions.astype(jnp.float32)[:, None] * frequency[None, :]
    cosine_table = jnp.cos(angles)
    sine_table = jnp.sin(angles)
    return (
        jnp.concatenate([cosine_table, cosine_table], -1),
        jnp.concatenate([sine_table, sine_table], -1),
    )


def rotate(values):
    middle = values.shape[-1] // 2
    return jnp.concatenate([-values[..., middle:], values[..., :middle]], -1)


def rotate_back(values):
    middle = values.shape[-1] // 2
    return jnp.concatenate([values[..., middle:], -values[..., :middle]], -1)


def norm_parts(values):
    scaling = lax.rsqrt(jnp.mean(values * values, -1, keepdims=True) + EPSILON)
    return (values * scaling, scaling)


def norm_back(grad_normed, normed_hat, scaling, gains):
    scaled = grad_normed * gains
    return scaling * (scaled - normed_hat * jnp.mean(scaled * normed_hat, -1, keepdims=True))


def contract_rows(left, right):
    return lax.dot_general(
        left, right, (((0,), (0,)), ((), ())), preferred_element_type=jnp.float32
    )


def contract_cols(left, right):
    return lax.dot_general(
        left, right, (((1,), (1,)), ((), ())), preferred_element_type=jnp.float32
    )


def block_scores(query_rows, key_token_rows, doc_row, start, width, factor):
    scores = (
        jnp.einsum("qgrd,kgd->grqk", query_rows, key_token_rows, preferred_element_type=jnp.float32)
        * factor
    )
    query_index = start + jnp.arange(width)
    key_index = jnp.arange(key_token_rows.shape[0])
    allowed = (doc_row[start : start + width, None] == doc_row[None, :]) & (
        key_index[None, :] <= query_index[:, None]
    )
    return jnp.where(allowed, scores, MASKED)


def on_device(
    tokens,
    documents,
    cotangent,
    attn_gain,
    query_gain,
    key_norm_scale,
    query_weight,
    key_projection,
    value_projection,
    output_weight,
    mlp_gain,
    gate_weight,
    up_weight,
    down_weight,
):
    rows = tokens.shape[0]
    seqs, seq_length = documents.shape
    head_size = HEAD_WIDTH
    local_heads = QUERY_HEADS // lax.axis_size("mp")
    device_groups = KEY_VALUE_HEADS // lax.axis_size("mp")
    query_group = QUERY_HEADS // KEY_VALUE_HEADS
    block = min(512, seq_length)
    factor = head_size ** (-0.5)
    share = rows // lax.axis_size("mp")
    offset = lax.axis_index("mp") * share

    def take(values):
        return lax.dynamic_slice_in_dim(values, offset, share, 0)

    attn_parts = (
        lax.all_gather(attn_gain.astype(jnp.bfloat16), "dp", axis=0, tiled=True),
        lax.all_gather(query_gain.astype(jnp.bfloat16), "dp", axis=0, tiled=True),
        lax.all_gather(key_norm_scale.astype(jnp.bfloat16), "dp", axis=0, tiled=True),
        lax.all_gather(query_weight.astype(jnp.bfloat16), "dp", axis=0, tiled=True),
        lax.all_gather(key_projection.astype(jnp.bfloat16), "dp", axis=0, tiled=True),
        lax.all_gather(value_projection.astype(jnp.bfloat16), "dp", axis=0, tiled=True),
        lax.all_gather(output_weight.astype(jnp.bfloat16), "dp", axis=1, tiled=True),
    )
    gain_one = attn_parts[0].astype(jnp.float32)
    gain_query = attn_parts[1].astype(jnp.float32)
    gain_key = attn_parts[2].astype(jnp.float32)
    query_mat, key_mat, value_mat, output_mat = (
        attn_parts[3],
        attn_parts[4],
        attn_parts[5],
        attn_parts[6],
    )
    mlp_parts = (
        lax.all_gather(mlp_gain.astype(jnp.bfloat16), "dp", axis=0, tiled=True),
        lax.all_gather(gate_weight.astype(jnp.bfloat16), "dp", axis=0, tiled=True),
        lax.all_gather(up_weight.astype(jnp.bfloat16), "dp", axis=0, tiled=True),
        lax.all_gather(down_weight.astype(jnp.bfloat16), "dp", axis=1, tiled=True),
    )
    gain_two = mlp_parts[0].astype(jnp.float32)
    gate_mat, up_mat, down_mat = (mlp_parts[1], mlp_parts[2], mlp_parts[3])
    inputs = tokens.astype(jnp.float32)
    hat_one, inv_one = norm_parts(inputs)
    normed_one = (hat_one * gain_one).astype(jnp.bfloat16)
    query_raw = jnp.dot(normed_one, query_mat, preferred_element_type=jnp.float32)
    key_unnormed = jnp.dot(normed_one, key_mat, preferred_element_type=jnp.float32)
    value_token_rows = jnp.dot(normed_one, value_mat, preferred_element_type=jnp.float32).astype(
        jnp.bfloat16
    )
    positions = doc_positions(documents).reshape(rows)
    cosine_table, sine_table = rope_tables(positions, head_size)
    cosine_table = cosine_table[:, None, :]
    sine_table = sine_table[:, None, :]
    query_hat, query_inv = norm_parts(query_raw.reshape(rows, local_heads, head_size))
    key_hat, key_inv = norm_parts(key_unnormed.reshape(rows, device_groups, head_size))
    query_normed = query_hat * gain_query
    key_normed = key_hat * gain_key
    query_rows = (query_normed * cosine_table + rotate(query_normed) * sine_table).astype(
        jnp.bfloat16
    )
    key_token_rows = (key_normed * cosine_table + rotate(key_normed) * sine_table).astype(
        jnp.bfloat16
    )
    query_seq = query_rows.reshape(seqs, seq_length, device_groups, query_group, head_size)
    key_seq = key_token_rows.reshape(seqs, seq_length, device_groups, head_size)
    value_seq = value_token_rows.reshape(seqs, seq_length, device_groups, head_size)

    def attend_forward(items):
        seq_queries, seq_keys, seq_values, doc_row = items
        outputs = []
        log_totals = []
        for start in range(0, seq_length, block):
            scores = block_scores(
                seq_queries[start : start + block], seq_keys, doc_row, start, block, factor
            )
            highest = jnp.max(scores, -1, keepdims=True)
            exponent = jnp.exp(scores - highest)
            totals = jnp.sum(exponent, -1, keepdims=True)
            weights_block = (exponent / totals).astype(jnp.bfloat16)
            outputs.append(
                jnp.einsum(
                    "grqk,kgd->qgrd", weights_block, seq_values, preferred_element_type=jnp.float32
                )
            )
            log_totals.append(highest + jnp.log(totals))
        return (jnp.concatenate(outputs, 0), jnp.concatenate(log_totals, 2))

    attention_output, log_total = lax.map(
        attend_forward, (query_seq, key_seq, value_seq, documents)
    )
    attended_flat = attention_output.reshape(rows, local_heads * head_size).astype(jnp.bfloat16)
    attn_part = jnp.dot(attended_flat, output_mat, preferred_element_type=jnp.float32)
    hidden = inputs + lax.psum(attn_part, "mp")
    hat_two, inv_two = norm_parts(hidden)
    normed_two = (hat_two * gain_two).astype(jnp.bfloat16)
    hidden_share = take(hidden)
    gate_pre = jnp.dot(normed_two, gate_mat, preferred_element_type=jnp.float32)
    up_pre = jnp.dot(normed_two, up_mat, preferred_element_type=jnp.float32)
    sigmoid = jax.nn.sigmoid(gate_pre)
    swish = gate_pre * sigmoid
    active = (swish * up_pre).astype(jnp.bfloat16)
    mlp_part = jnp.dot(active, down_mat, preferred_element_type=jnp.float32)
    layer_output = (
        hidden_share + take(lax.psum(mlp_part.astype(jnp.bfloat16), "mp").astype(jnp.float32))
    ).astype(jnp.bfloat16)
    back_gain_one, back_gain_query, back_gain_key = (gain_one, gain_query, gain_key)
    back_query, back_key, back_value, back_output = (query_mat, key_mat, value_mat, output_mat)
    back_gate, back_up, back_down = (gate_mat, up_mat, down_mat)
    grad_out = cotangent.astype(jnp.float32)
    grad_active = contract_cols(cotangent, back_down)
    down_grad = contract_rows(active, cotangent)
    grad_gate = (grad_active * up_pre * sigmoid * (1.0 + gate_pre * (1.0 - sigmoid))).astype(
        jnp.bfloat16
    )
    grad_up = (grad_active * swish).astype(jnp.bfloat16)
    gate_grad = contract_rows(normed_two, grad_gate)
    up_grad = contract_rows(normed_two, grad_up)
    normed_two_part = contract_cols(grad_gate, back_gate) + contract_cols(grad_up, back_up)
    normed_two_grad = lax.psum(normed_two_part.astype(jnp.bfloat16), "mp").astype(jnp.float32)
    mlp_gain_part = jnp.sum(normed_two_grad * hat_two, 0)
    grad_hidden = grad_out + norm_back(normed_two_grad, hat_two, inv_two, gain_two)
    grad_hidden_low = grad_hidden.astype(jnp.bfloat16)
    grad_hidden_share = take(grad_hidden)
    output_grad = contract_rows(attended_flat, grad_hidden_low)
    grad_attended = contract_cols(grad_hidden_low, back_output).astype(jnp.bfloat16)
    grad_attended_seq = grad_attended.reshape(
        seqs, seq_length, device_groups, query_group, head_size
    )

    def attend_backward(items):
        seq_queries, seq_keys, seq_values, doc_row, seq_log_total, seq_grad = items
        query_grads = []
        key_grad = jnp.zeros((seq_length, device_groups, head_size), jnp.float32)
        value_grad = jnp.zeros((seq_length, device_groups, head_size), jnp.float32)
        for start in range(0, seq_length, block):
            block_queries = seq_queries[start : start + block]
            block_grad = seq_grad[start : start + block]
            scores = block_scores(block_queries, seq_keys, doc_row, start, block, factor)
            weights_block = jnp.exp(scores - seq_log_total[:, :, start : start + block])
            grad_weights = jnp.einsum(
                "qgrd,kgd->grqk", block_grad, seq_values, preferred_element_type=jnp.float32
            )
            inner = jnp.sum(weights_block * grad_weights, -1, keepdims=True)
            grad_scores = (weights_block * (grad_weights - inner)).astype(jnp.bfloat16)
            query_grads.append(
                jnp.einsum(
                    "grqk,kgd->qgrd", grad_scores, seq_keys, preferred_element_type=jnp.float32
                )
                * factor
            )
            key_grad = (
                key_grad
                + jnp.einsum(
                    "grqk,qgrd->kgd", grad_scores, block_queries, preferred_element_type=jnp.float32
                )
                * factor
            )
            value_grad = value_grad + jnp.einsum(
                "grqk,qgrd->kgd",
                weights_block.astype(jnp.bfloat16),
                block_grad,
                preferred_element_type=jnp.float32,
            )
        return (jnp.concatenate(query_grads, 0), key_grad, value_grad)

    query_rot_grad, key_rot_grad, value_seq_grad = lax.map(
        attend_backward, (query_seq, key_seq, value_seq, documents, log_total, grad_attended_seq)
    )
    query_rot_grad = query_rot_grad.reshape(rows, local_heads, head_size)
    key_rot_grad = key_rot_grad.reshape(rows, device_groups, head_size)
    query_norm_grad = query_rot_grad * cosine_table + rotate_back(query_rot_grad * sine_table)
    key_norm_grad = key_rot_grad * cosine_table + rotate_back(key_rot_grad * sine_table)
    query_gain_part = jnp.sum(query_norm_grad * query_hat, (0, 1))
    key_gain_part = jnp.sum(key_norm_grad * key_hat, (0, 1))
    query_raw_grad = (
        norm_back(query_norm_grad, query_hat, query_inv, back_gain_query)
        .reshape(rows, local_heads * head_size)
        .astype(jnp.bfloat16)
    )
    key_raw_grad = (
        norm_back(key_norm_grad, key_hat, key_inv, back_gain_key)
        .reshape(rows, device_groups * head_size)
        .astype(jnp.bfloat16)
    )
    value_raw_grad = value_seq_grad.reshape(rows, device_groups * head_size).astype(jnp.bfloat16)
    query_grad = contract_rows(normed_one, query_raw_grad)
    key_grad = contract_rows(normed_one, key_raw_grad)
    value_grad = contract_rows(normed_one, value_raw_grad)
    normed_one_part = (
        contract_cols(query_raw_grad, back_query)
        + contract_cols(key_raw_grad, back_key)
        + contract_cols(value_raw_grad, back_value)
    )
    hat_one_share = take(hat_one)
    inv_one_share = take(inv_one)
    normed_one_grad, query_gain_sum, key_gain_sum = (
        lax.psum(normed_one_part.astype(jnp.bfloat16), "mp").astype(jnp.float32),
        lax.psum(query_gain_part.astype(jnp.bfloat16), "mp").astype(jnp.float32),
        lax.psum(key_gain_part.astype(jnp.bfloat16), "mp").astype(jnp.float32),
    )
    attn_gain_total = jnp.sum(normed_one_grad * hat_one, 0)
    input_grad = grad_hidden_share + norm_back(
        take(normed_one_grad), hat_one_share, inv_one_share, back_gain_one
    )
    attn_grads = (
        lax.psum_scatter(
            attn_gain_total.astype(jnp.bfloat16), "dp", scatter_dimension=0, tiled=True
        ).astype(jnp.float32),
        lax.psum_scatter(
            query_gain_sum.astype(jnp.bfloat16), "dp", scatter_dimension=0, tiled=True
        ).astype(jnp.float32),
        lax.psum_scatter(
            key_gain_sum.astype(jnp.bfloat16), "dp", scatter_dimension=0, tiled=True
        ).astype(jnp.float32),
        lax.psum_scatter(
            query_grad.astype(jnp.bfloat16), "dp", scatter_dimension=0, tiled=True
        ).astype(jnp.float32),
        lax.psum_scatter(
            key_grad.astype(jnp.bfloat16), "dp", scatter_dimension=0, tiled=True
        ).astype(jnp.float32),
        lax.psum_scatter(
            value_grad.astype(jnp.bfloat16), "dp", scatter_dimension=0, tiled=True
        ).astype(jnp.float32),
        lax.psum_scatter(
            output_grad.astype(jnp.bfloat16), "dp", scatter_dimension=1, tiled=True
        ).astype(jnp.float32),
    )
    mlp_grads = (
        lax.psum_scatter(
            mlp_gain_part.astype(jnp.bfloat16), "dp", scatter_dimension=0, tiled=True
        ).astype(jnp.float32),
        lax.psum_scatter(
            gate_grad.astype(jnp.bfloat16), "dp", scatter_dimension=0, tiled=True
        ).astype(jnp.float32),
        lax.psum_scatter(
            up_grad.astype(jnp.bfloat16), "dp", scatter_dimension=0, tiled=True
        ).astype(jnp.float32),
        lax.psum_scatter(
            down_grad.astype(jnp.bfloat16), "dp", scatter_dimension=1, tiled=True
        ).astype(jnp.float32),
    )
    return (
        layer_output,
        input_grad,
        attn_grads[0],
        attn_grads[1],
        attn_grads[2],
        attn_grads[3],
        attn_grads[4],
        attn_grads[5],
        attn_grads[6],
        mlp_grads[0],
        mlp_grads[1],
        mlp_grads[2],
        mlp_grads[3],
    )


def solution(mesh):
    in_specs = (
        P("dp", None),
        P("dp", None),
        P("dp", None),
        P("dp"),
        P("dp"),
        P("dp"),
        P("dp", "mp"),
        P("dp", "mp"),
        P("dp", "mp"),
        P("mp", "dp"),
        P("dp"),
        P("dp", "mp"),
        P("dp", "mp"),
        P("mp", "dp"),
    )
    out_specs = (
        P(("dp", "mp"), None),
        P(("dp", "mp"), None),
        P("dp"),
        P("dp"),
        P("dp"),
        P("dp", "mp"),
        P("dp", "mp"),
        P("dp", "mp"),
        P("mp", "dp"),
        P("dp"),
        P("dp", "mp"),
        P("dp", "mp"),
        P("mp", "dp"),
    )
    return jax.shard_map(
        on_device, mesh=mesh, in_specs=in_specs, out_specs=out_specs, check_vma=False
    )
```

profile of v0, /device:TPU:0, one launch (start us, length us, event | category | flops | bytes accessed | tf_op | source)
XLA Modules:
  0.0 1635.1 jit_solution(17745862805396485269)
XLA Ops:
  16.6 22.3 %all-gather = bf16[8,1,256]{2,1,0:T(2,128)(2,1)S(1)} all-gather(bf16[1,1,256]{2,1,0:T(2,128)(2,1)S(1)} %reshape.304), channel_id=1, replica_groups=mesh['dp'=8,'mp'=4] {'dp'}, dimensions={0}, use_global_device_ids=true | all-gather | bytes 4608 | tf_op jit(solution)/shard_map/all_gather | solution.py:114
  43.8 17.2 %all-reduce.7 = (bf16[128]{0:T(256)(128)(2,1)S(1)}, bf16[128]{0:T(256)(128)(2,1)S(1)}) all-reduce(bf16[128]{0:T(256)(128)(2,1)S(1)} %dynamic-update-slice, bf16[128]{0:T(256)(128)(2,1)S(1)} %dynamic-update-slice.1), channel_id=1, replica_groups=mesh['dp'=8,'mp'=4] {'dp'}, use_global_device_ids=true, to_apply=%add | all-reduce | flops 256 | bytes 1024
  63.7 4.0 multiply_reduce_fusion.7
  69.1 26.4 %all-gather.10.cloned.1.call-done = bf16[2048,256]{1,0:T(8,128)(2,1)} async-done(((bf16[256,256]{1,0:T(8,128)(2,1)}), bf16[2048,256]{1,0:T(8,128)(2,1)}) %all-gather.10.cloned.1.call-update) | async-done | bytes 1048592 | tf_op jit(solution)/shard_map/all_gather | solution.py:119
  95.5 4.0 convolution_convert_fusion.8
  99.5 46.8 %all-gather.14.cloned.1.call-done = bf16[2048,512]{1,0:T(8,128)(2,1)} async-done(((bf16[256,512]{1,0:T(8,128)(2,1)}), bf16[2048,512]{1,0:T(8,128)(2,1)}) %all-gather.14.cloned.1.call-update) | async-done | bytes 2097168 | tf_op jit(solution)/shard_map/all_gather | solution.py:117
  146.3 5.4 multiply_reduce_fusion.4
  164.0 34.4 %all-gather.16.cloned.1.call-done = bf16[512,2048]{1,0:T(8,128)(2,1)} async-done(((bf16[512,256]{1,0:T(8,128)(2,1)}), bf16[512,2048]{1,0:T(8,128)(2,1)}) %all-gather.16.cloned.1.call-update) | async-done | bytes 2097168 | tf_op jit(solution)/shard_map/all_gather | solution.py:120
  198.4 7.2 fusion.77
  212.0 17.4 %all-gather.1 = bf16[8,1,256]{2,1,0:T(2,128)(2,1)S(1)} all-gather(bf16[1,1,256]{2,1,0:T(2,128)(2,1)S(1)} %reshape.306), channel_id=1, replica_groups=mesh['dp'=8,'mp'=4] {'dp'}, dimensions={0}, use_global_device_ids=true | all-gather | bytes 4608 | tf_op jit(solution)/shard_map/all_gather | solution.py:132
  230.0 126.9 %all-reduce.14.cloned.1.call-done = f32[1024,2048]{1,0:T(8,128)} async-done(((f32[1024,2048]{1,0:T(8,128)}), f32[1024,2048]{1,0:T(8,128)}) %all-reduce.14.cloned.1.call-update) | async-done | bytes 8388624 | tf_op jit(solution)/shard_map/psum | solution.py:190
  356.8 5.7 multiply_reduce_fusion.1
  362.6 3.3 copy-done.2
  368.6 90.1 %all-gather.18.cloned.1.call-done = bf16[2048,1536]{1,0:T(8,128)(2,1)} async-done(((bf16[256,1536]{1,0:T(8,128)(2,1)}), bf16[2048,1536]{1,0:T(8,128)(2,1)}) %all-gather.18.cloned.1.call-update) | async-done | bytes 6291472 | tf_op jit(solution)/shard_map/all_gather | solution.py:133
  458.7 11.9 fusion.78
  470.6 88.1 %all-gather.20.cloned.1.call-done = bf16[2048,1536]{1,0:T(8,128)(2,1)} async-done(((bf16[256,1536]{1,0:T(8,128)(2,1)}), bf16[2048,1536]{1,0:T(8,128)(2,1)}) %all-gather.20.cloned.1.call-update) | async-done | bytes 6291472 | tf_op jit(solution)/shard_map/all_gather | solution.py:134
  558.7 11.7 fusion.79
  570.4 89.1 %all-gather.22.cloned.1.call-done = bf16[1536,2048]{1,0:T(8,128)(2,1)} async-done(((bf16[1536,256]{1,0:T(8,128)(2,1)}), bf16[1536,2048]{1,0:T(8,128)(2,1)}) %all-gather.22.cloned.1.call-update) | async-done | bytes 6291472 | tf_op jit(solution)/shard_map/all_gather | solution.py:135
  659.4 16.4 %multiply_convert_fusion.2 = (bf16[1024,1536]{1,0:T(8,128)(2,1)}, bf16[1024,1536]{1,0:T(8,128)(2,1)S(1)}, bf16[1024,1536]{1,0:T(8,128)(2,1)}) fusion(f32[1024,1536]{1,0:T(8,128)} %fusion.78, f32[1024,1536]{1,0:T(8,128)} %fusion.79, bf16[1024,2048]{1,0:T(8,128)(2,1)} %param.16, bf16[1536,2048]{1,0:T(8,128)(2,1)} %all-gather.22.cloned.1.call-done), kind=kOutput, calls=%fused_computation.43 | convolution fusion | flops 6466043904 | bytes 32505856 | tf_op jit(solution)/shard_map/dot_general | solution.py:65
  675.8 10.0 fusion.80
  685.8 10.2 add_convert_fusion.1
  696.2 11.3 convolution_convert_fusion.3
  707.5 72.4 %all-reduce.16.cloned.1.call-done = bf16[1024,2048]{1,0:T(8,128)(2,1)} async-done(((bf16[1024,2048]{1,0:T(8,128)(2,1)}), bf16[1024,2048]{1,0:T(8,128)(2,1)}) %all-reduce.16.cloned.1.call-update) | async-done | bytes 4194320 | tf_op jit(solution)/shard_map/psum | solution.py:216
  779.9 6.0 fusion.5
  787.0 5.0 fusion.4
  800.2 5.0 fusion.7
  805.2 5.1 fusion.9
  828.8 4.9 convolution_convert_fusion.6
  833.9 5.1 fusion.33
  843.4 3.3 add_convert_fusion
  846.8 4.9 convolution_convert_fusion.7
  851.8 6.5 convolution_convert_fusion.5
  858.6 7.1 convolution_convert_fusion.4
  865.8 11.5 convolution_convert_fusion.2
  879.2 11.0 convolution_convert_fusion.1
  892.1 10.9 convolution_convert_fusion
  906.1 146.2 %all-reduce.18.cloned.1.call-done = (bf16[1024,2048]{1,0:T(8,128)(2,1)}, bf16[1024,2048]{1,0:T(8,128)(2,1)}) async-done(((bf16[1024,2048]{1,0:T(8,128)(2,1)}, bf16[1024,2048]{1,0:T(8,128)(2,1)}), (bf16[1024,2048]{1,0:T(8,128)(2,1)}, bf16[1024,2048]{1,0:T(8,128)(2,1)})) %all-reduce.18.cloned.1.call-update) | async-done | bytes 8388624 | tf_op jit(solution)/shard_map/psum | solution.py:201
  1052.2 6.5 multiply_reduce_fusion
  1058.8 22.0 %all-reduce.6 = (bf16[2048]{0:T(1024)(128)(2,1)S(1)}, bf16[128]{0:T(256)(128)(2,1)S(1)}, bf16[128]{0:T(256)(128)(2,1)S(1)}, bf16[2048]{0:T(1024)(128)(2,1)S(1)}) all-reduce(bf16[2048]{0:T(1024)(128)(2,1)S(1)} %get-tuple-element.84, bf16[128]{0:T(256)(128)(2,1)S(1)} %reduce_sum.170, ...), channel_id=2, replica_groups=mesh['dp'=8,'mp'=4] {'dp'}, use_global_device_ids=true, to_apply=%region_21.22.clone | all-reduce | flops 4352 | bytes 17408
  1081.0 38.8 %reduce-scatter.10.cloned.1.call-done = bf16[256,256]{1,0:T(8,128)(2,1)} async-done(((bf16[2048,256]{1,0:T(8,128)(2,1)}), bf16[256,256]{1,0:T(8,128)(2,1)}) %reduce-scatter.10.cloned.1.call-update) | async-done | bytes 131088 | tf_op jit(solution)/shard_map/reduce_scatter | solution.py:315
  1121.4 5.6 all-reduce.8
  1127.0 6.7 convert_element_type.272
  1134.7 56.6 %reduce-scatter.8.cloned.1.call-done = bf16[256,512]{1,0:T(8,128)(2,1)} async-done(((bf16[2048,512]{1,0:T(8,128)(2,1)}), bf16[256,512]{1,0:T(8,128)(2,1)}) %reduce-scatter.8.cloned.1.call-update) | async-done | bytes 262160 | tf_op jit(solution)/shard_map/reduce_scatter | solution.py:312
  1193.1 69.3 %reduce-scatter.14.cloned.1.call-done = bf16[512,256]{1,0:T(8,128)(2,1)} async-done(((bf16[512,2048]{1,0:T(8,128)(2,1)}), bf16[512,256]{1,0:T(8,128)(2,1)}) %reduce-scatter.14.cloned.1.call-update) | async-done | bytes 262160 | tf_op jit(solution)/shard_map/reduce_scatter | solution.py:321
  1267.3 6.0 multiply_add_fusion
  1273.3 110.0 %reduce-scatter.16.cloned.1.call-done = bf16[256,1536]{1,0:T(8,128)(2,1)} async-done(((bf16[2048,1536]{1,0:T(8,128)(2,1)}), bf16[256,1536]{1,0:T(8,128)(2,1)}) %reduce-scatter.16.cloned.1.call-update) | async-done | bytes 786448 | tf_op jit(solution)/shard_map/reduce_scatter | solution.py:329
  1385.7 118.5 %reduce-scatter.18.cloned.1.call-done = bf16[256,1536]{1,0:T(8,128)(2,1)} async-done(((bf16[2048,1536]{1,0:T(8,128)(2,1)}), bf16[256,1536]{1,0:T(8,128)(2,1)}) %reduce-scatter.18.cloned.1.call-update) | async-done | bytes 786448 | tf_op jit(solution)/shard_map/reduce_scatter | solution.py:332
  1506.7 119.0 %reduce-scatter.20.cloned.1.call-done = bf16[1536,256]{1,0:T(8,128)(2,1)} async-done(((bf16[1536,2048]{1,0:T(8,128)(2,1)}), bf16[1536,256]{1,0:T(8,128)(2,1)}) %reduce-scatter.20.cloned.1.call-update) | async-done | bytes 786448 | tf_op jit(solution)/shard_map/reduce_scatter | solution.py:335
  (257 shorter events, 94.1 us)
Async XLA Ops:
  7.2 34.9 %copy-start.45 = (u32[32]{0:T(128)S(1)}, u32[32]{0:T(128)}, u32[]{:S(2)}) copy-start(u32[32]{0:T(128)} %constant.106) | copy-start | bytes 388
  7.2 34.8 %copy-start.50 = (f32[16]{0:T(128)S(1)}, f32[16]{0:T(128)}, u32[]{:S(2)}) copy-start(f32[16]{0:T(128)} %param.19) | copy-start | bytes 196
  7.2 34.8 %copy-start.51 = (f32[16]{0:T(128)S(1)}, f32[16]{0:T(128)}, u32[]{:S(2)}) copy-start(f32[16]{0:T(128)} %param.18) | copy-start | bytes 196
  7.2 56.4 %all-gather.12.cloned.1.call-start = ((), (), s32[]{:S(2)}) async-start(), calls=%async_computation.8 | async-start | bytes 1179648 | tf_op jit(solution)/shard_map/all_gather | solution.py:118
  8.9 86.6 %all-gather.10.cloned.1.call-start = ((), (), s32[]{:S(2)}) async-start(), calls=%async_computation.7 | async-start | bytes 1179648 | tf_op jit(solution)/shard_map/all_gather | solution.py:119
  10.6 52.3 %copy-start.39 = (s32[1,1024]{1,0:T(1,128)S(1)}, s32[1,1024]{1,0:T(1,128)}, u32[]{:S(2)}) copy-start(s32[1,1024]{1,0:T(1,128)} %param.15) | copy-start | bytes 12292
  10.6 135.7 %all-gather.14.cloned.1.call-start = ((), (), s32[]{:S(2)}) async-start(), calls=%async_computation.9 | async-start | bytes 2359296 | tf_op jit(solution)/shard_map/all_gather | solution.py:117
  12.5 185.9 %all-gather.16.cloned.1.call-start = ((), (), s32[]{:S(2)}) async-start(), calls=%async_computation.10 | async-start | bytes 2359296 | tf_op jit(solution)/shard_map/all_gather | solution.py:120
  14.3 342.5 %all-reduce.14.cloned.1.call-start = ((), (), s32[]{:S(2)}) async-start(), calls=%async_computation.11 | async-start | bytes 16777216 | tf_op jit(solution)/shard_map/psum | solution.py:190
  38.9 107.4 %copy-start.37 = (f32[8,1,256]{2,1,0:T(1,128)}, f32[8,1,256]{2,1,0:T(1,128)S(1)}, u32[]{:S(2)}) copy-start(f32[8,1,256]{2,1,0:T(1,128)S(1)} %convert_element_type.295) | copy-start | bytes 24580
  42.0 104.3 %copy-start.40 = (f32[1024]{0:T(1024)}, f32[1024]{0:T(1024)S(1)}, u32[]{:S(2)}) copy-start(f32[1024]{0:T(1024)S(1)} %add_rsqrt_fusion.3) | copy-start | bytes 12292
  61.0 7.0 copy-start.43
  62.9 89.5 %copy-start.7 = (f32[1024,128]{0,1:T(8,128)}, f32[1024,128]{0,1:T(8,128)S(1)}, u32[]{:S(2)}) copy-start(f32[1024,128]{0,1:T(8,128)S(1)} %pad_maximum_fusion.4) | copy-start | bytes 1572868
  62.9 89.4 %copy-start.9 = (f32[1024,128]{0,1:T(8,128)}, f32[1024,128]{0,1:T(8,128)S(1)}, u32[]{:S(2)}) copy-start(f32[1024,128]{0,1:T(8,128)S(1)} %pad_maximum_fusion.5) | copy-start | bytes 1572868
  69.1 88.1 %copy-start.16 = (bf16[1024,2,128,1]{0,2,3,1:T(8,128)(2,1)}, bf16[1024,2,128,1]{0,2,3,1:T(8,128)(2,1)S(1)}, u32[]{:S(2)}) copy-start(bf16[1024,2,128,1]{0,2,3,1:T(8,128)(2,1)S(1)} %fusion.64) | copy-start | bytes 1572868
  153.9 3.3 copy-start.20
  155.6 4.5 copy-start
  163.9 41.7 %copy-start.33 = (bf16[1024,2,2,128]{0,3,2,1:T(8,128)(2,1)}, bf16[1024,2,2,128]{0,3,2,1:T(8,128)(2,1)S(1)}, u32[]{:S(2)}) copy-start(bf16[1024,2,2,128]{0,3,2,1:T(8,128)(2,1)S(1)} %pad_maximum_fusion.3) | copy-start | bytes 3145732
  205.6 6.3 copy-start.49
  205.6 253.0 %all-gather.18.cloned.1.call-start = ((), (), s32[]{:S(2)}) async-start(), calls=%async_computation.12 | async-start | bytes 7077888 | tf_op jit(solution)/shard_map/all_gather | solution.py:133
  208.0 350.7 %all-gather.20.cloned.1.call-start = ((), (), s32[]{:S(2)}) async-start(), calls=%async_computation.13 | async-start | bytes 7077888 | tf_op jit(solution)/shard_map/all_gather | solution.py:134
  210.8 448.6 %all-gather.22.cloned.1.call-start = ((), (), s32[]{:S(2)}) async-start(), calls=%async_computation.14 | async-start | bytes 7077888 | tf_op jit(solution)/shard_map/all_gather | solution.py:135
  211.9 568.0 %all-reduce.16.cloned.1.call-start = ((), (), s32[]{:S(2)}) async-start(), calls=%async_computation.15 | async-start | bytes 8388608 | tf_op jit(solution)/shard_map/psum | solution.py:216
  675.8 10.0 copy-start.52
  675.8 10.0 copy-start.46
  696.1 208.3 %reduce-scatter.12.cloned.1.call-start = ((), (), s32[]{:S(2)}) async-start(), calls=%async_computation.18 | async-start | bytes 1179648 | tf_op jit(solution)/shard_map/reduce_scatter | solution.py:318
  779.9 6.0 copy-start.12
  779.9 7.1 copy-start.24
  779.9 15.5 slice-start
  787.0 5.0 copy-start.48
  787.0 8.5 slice-start.1
  792.0 3.3 copy-start.15
  795.5 4.4 slice-start.2
  805.2 5.1 copy-start.21
  814.0 12.5 copy-start.13
  820.4 6.2 copy-start.14
  828.7 5.2 copy-start.42
  833.7 218.6 %all-reduce.18.cloned.1.call-start = ((), (), s32[]{:S(2)}) async-start(), calls=%async_computation.23 | async-start | bytes 16777216 | tf_op jit(solution)/shard_map/psum | solution.py:201
  833.9 5.1 copy-start.22
  833.9 5.4 copy-start.29
  846.7 5.0 copy-start.32
  846.7 273.0 %reduce-scatter.10.cloned.1.call-start = ((), (), s32[]{:S(2)}) async-start(), calls=%async_computation.17 | async-start | bytes 1179648 | tf_op jit(solution)/shard_map/reduce_scatter | solution.py:315
  851.7 6.9 copy-start.34
  851.7 339.5 %reduce-scatter.8.cloned.1.call-start = ((), (), s32[]{:S(2)}) async-start(), calls=%async_computation.16 | async-start | bytes 2359296 | tf_op jit(solution)/shard_map/reduce_scatter | solution.py:312
  858.3 404.0 %reduce-scatter.14.cloned.1.call-start = ((), (), s32[]{:S(2)}) async-start(), calls=%async_computation.19 | async-start | bytes 2359296 | tf_op jit(solution)/shard_map/reduce_scatter | solution.py:321
  865.7 517.5 %reduce-scatter.16.cloned.1.call-start = ((), (), s32[]{:S(2)}) async-start(), calls=%async_computation.20 | async-start | bytes 7077888 | tf_op jit(solution)/shard_map/reduce_scatter | solution.py:329
  877.3 627.0 %reduce-scatter.18.cloned.1.call-start = ((), (), s32[]{:S(2)}) async-start(), calls=%async_computation.21 | async-start | bytes 7077888 | tf_op jit(solution)/shard_map/reduce_scatter | solution.py:332
  890.2 735.5 %reduce-scatter.20.cloned.1.call-start = ((), (), s32[]{:S(2)}) async-start(), calls=%async_computation.22 | async-start | bytes 7077888 | tf_op jit(solution)/shard_map/reduce_scatter | solution.py:335
  (28 other events, 52.7 us)
Sparse Core Ops, SparseCore 0:
  10.7 42.9 all-gather.11
  56.4 39.0 all-gather.9
  98.2 48.0 all-gather.13
  148.8 49.5 all-gather.15
  205.8 151.0 all-reduce.13
  359.5 99.1 all-gather.17
  461.4 97.1 all-gather.19
  561.3 98.1 all-gather.21
  696.2 83.6 all-reduce.15
  833.8 63.5 reduce-scatter.11
  900.0 152.2 all-reduce.17
  1056.1 63.6 reduce-scatter.9
  1124.3 66.9 reduce-scatter.7
  1195.0 67.2 reduce-scatter.13
  1266.2 117.0 reduce-scatter.15
  1387.1 117.0 reduce-scatter.17
  1508.2 117.5 reduce-scatter.19
where the time goes:
time: 1650 us; the launch traced here: 1640 us
  waiting for transfers between devices  1230 us (75%)
  matrix products  182 us (11%)
  other arithmetic  98.9 us (6%)
  blocking collectives  84.5 us (5%)
  local copies, waits for them, and re-layouts  17.7 us (1%)
  between operations  17.4 us (1%)
    psum x1, waiting for transfers between devices, on_device(): lax.psum(mlp_part.astype(jnp.bfloat16), 'mp').astype(jnp.float32)  146 us
    psum x1, waiting for transfers between devices, on_device(): hidden = inputs + lax.psum(attn_part, 'mp')  127 us
    reduce_scatter x1, waiting for transfers between devices, on_device(): lax.psum_scatter(down_grad.astype(jnp.bfloat16), 'dp', scatter_dimension=...  119 us
    reduce_scatter x1, waiting for transfers between devices, on_device(): lax.psum_scatter(up_grad.astype(jnp.bfloat16), 'dp', scatter_dimension=0,...  119 us
    reduce_scatter x1, waiting for transfers between devices, on_device(): lax.psum_scatter(gate_grad.astype(jnp.bfloat16), 'dp', scatter_dimension=...  110 us
    all_gather x1, waiting for transfers between devices, on_device(): lax.all_gather(gate_weight.astype(jnp.bfloat16), 'dp', axis=0, tiled=True)  90.1 us
    all_gather x1, waiting for transfers between devices, on_device(): lax.all_gather(down_weight.astype(jnp.bfloat16), 'dp', axis=1, tiled=True)  89.1 us
    all_gather x1, waiting for transfers between devices, on_device(): lax.all_gather(up_weight.astype(jnp.bfloat16), 'dp', axis=0, tiled=True)  88.1 us
  transfers between devices with their start and end apart: 17, of which 15 were waited for; matrix products, arithmetic and copies ran while one was open for 11% of the time, Pallas kernels for 0%

commit v1 on v0

--- a/solution.py
+++ b/solution.py
@@ -1,3 +1,4 @@
+import functools
 import jax
 import jax.numpy as jnp
 from jax import lax
@@ -8,6 +9,13 @@
 HEAD_WIDTH = 128
 EPSILON = 1e-06
 MASKED = -1e30
+
+
+def make_figure_on(x_part, mesh_dim):
+    return lax.all_gather(x_part, mesh_dim).sum(axis=0)
+
+
+shards_set = functools.partial(make_figure_on, mesh_dim="mp")
 
 
 def doc_positions(documents):
@@ -187,7 +195,7 @@
     )
     attended_flat = attention_output.reshape(rows, local_heads * head_size).astype(jnp.bfloat16)
     attn_part = jnp.dot(attended_flat, output_mat, preferred_element_type=jnp.float32)
-    hidden = inputs + lax.psum(attn_part, "mp")
+    hidden = inputs + shards_set(attn_part)
     hat_two, inv_two = norm_parts(hidden)
     normed_two = (hat_two * gain_two).astype(jnp.bfloat16)
     hidden_share = take(hidden)

time: 1650 us -> 1690 us (1.024)
  other arithmetic: 98.9 us -> 125 us
  waiting for transfers between devices: 1230 us -> 1250 us
    all_gather x0 -> x1, waiting for transfers between devices: none -> 176 us  [make_figure_on(): return lax.all_gather(x_part, mesh_dim).sum(axis=0)]
    psum x1 -> x0, waiting for transfers between devices: 127 us -> none  [on_device(): hidden = inputs + lax.psum(attn_part, 'mp')]
    all_gather x1, waiting for transfers between devices: 90.1 us -> 63 us  [on_device(): lax.all_gather(gate_weight.astype(jnp.bfloat16), 'dp', axis=0, tiled=True)]
    reduce_sum x0 -> x1, other arithmetic: none -> 26.9 us  [make_figure_on(): return lax.all_gather(x_part, mesh_dim).sum(axis=0)]
  transfers between devices with their start and end apart: 17 -> 17, of which waited for: 15 -> 15; matrix products, arithmetic and copies ran while one was open for 11% -> 13% of each run, Pallas kernels for 0% -> 0%
where the time goes in v1:
time: 1690 us; the launch traced here: 1680 us
  waiting for transfers between devices  1250 us (74%)
  matrix products  182 us (11%)
  other arithmetic  125 us (7%)
  blocking collectives  84.8 us (5%)
  local copies, waits for them, and re-layouts  17.7 us (1%)
  between operations  17.5 us (1%)
    all_gather x1, waiting for transfers between devices, make_figure_on(): return lax.all_gather(x_part, mesh_dim).sum(axis=0)  176 us
    psum x1, waiting for transfers between devices, on_device(): lax.psum(mlp_part.astype(jnp.bfloat16), 'mp').astype(jnp.float32)  146 us
    reduce_scatter x1, waiting for transfers between devices, on_device(): lax.psum_scatter(down_grad.astype(jnp.bfloat16), 'dp', scatter_dimension=...  119 us
    reduce_scatter x1, waiting for transfers between devices, on_device(): lax.psum_scatter(up_grad.astype(jnp.bfloat16), 'dp', scatter_dimension=0,...  119 us
    reduce_scatter x1, waiting for transfers between devices, on_device(): lax.psum_scatter(gate_grad.astype(jnp.bfloat16), 'dp', scatter_dimension=...  110 us
    all_gather x1, waiting for transfers between devices, on_device(): lax.all_gather(down_weight.astype(jnp.bfloat16), 'dp', axis=1, tiled=True)  89 us
    all_gather x1, waiting for transfers between devices, on_device(): lax.all_gather(up_weight.astype(jnp.bfloat16), 'dp', axis=0, tiled=True)  88.3 us
    psum x1, waiting for transfers between devices, on_device(): lax.psum(normed_two_part.astype(jnp.bfloat16), 'mp').astype(jnp.float32)  72.4 us
  transfers between devices with their start and end apart: 17, of which 15 were waited for; matrix products, arithmetic and copies ran while one was open for 13% of the time, Pallas kernels for 0%

profile of v1, /device:TPU:0, one launch (start us, length us, event | category | flops | bytes accessed | tf_op | source)
XLA Modules:
  0.0 1683.8 jit_solution(16839996541469192181)
XLA Ops:
  16.6 22.3 %all-gather.1 = bf16[8,1,256]{2,1,0:T(2,128)(2,1)S(1)} all-gather(bf16[1,1,256]{2,1,0:T(2,128)(2,1)S(1)} %reshape.305), channel_id=1, replica_groups=mesh['dp'=8,'mp'=4] {'dp'}, dimensions={0}, use_global_device_ids=true | all-gather | bytes 4608 | tf_op jit(solution)/shard_map/all_gather | solution.py:122
  43.8 17.2 %all-reduce.7 = (bf16[128]{0:T(256)(128)(2,1)S(1)}, bf16[128]{0:T(256)(128)(2,1)S(1)}) all-reduce(bf16[128]{0:T(256)(128)(2,1)S(1)} %dynamic-update-slice, bf16[128]{0:T(256)(128)(2,1)S(1)} %dynamic-update-slice.1), channel_id=1, replica_groups=mesh['dp'=8,'mp'=4] {'dp'}, use_global_device_ids=true, to_apply=%add | all-reduce | flops 256 | bytes 1024
  63.7 4.0 multiply_reduce_fusion.7
  69.1 26.4 %all-gather.12.cloned.1.call-done = bf16[2048,256]{1,0:T(8,128)(2,1)} async-done(((bf16[256,256]{1,0:T(8,128)(2,1)}), bf16[2048,256]{1,0:T(8,128)(2,1)}) %all-gather.12.cloned.1.call-update) | async-done | bytes 1048592 | tf_op jit(solution)/shard_map/all_gather | solution.py:127
  95.5 4.0 convolution_convert_fusion.8
  99.5 46.8 %all-gather.16.cloned.1.call-done = bf16[2048,512]{1,0:T(8,128)(2,1)} async-done(((bf16[256,512]{1,0:T(8,128)(2,1)}), bf16[2048,512]{1,0:T(8,128)(2,1)}) %all-gather.16.cloned.1.call-update) | async-done | bytes 2097168 | tf_op jit(solution)/shard_map/all_gather | solution.py:125
  146.3 5.4 multiply_reduce_fusion.4
  163.9 34.5 %all-gather.18.cloned.1.call-done = bf16[512,2048]{1,0:T(8,128)(2,1)} async-done(((bf16[512,256]{1,0:T(8,128)(2,1)}), bf16[512,2048]{1,0:T(8,128)(2,1)}) %all-gather.18.cloned.1.call-update) | async-done | bytes 2097168 | tf_op jit(solution)/shard_map/all_gather | solution.py:128
  198.4 7.2 fusion.77
  211.7 17.7 %all-gather.2 = bf16[8,1,256]{2,1,0:T(2,128)(2,1)S(1)} all-gather(bf16[1,1,256]{2,1,0:T(2,128)(2,1)S(1)} %reshape.307), channel_id=1, replica_groups=mesh['dp'=8,'mp'=4] {'dp'}, dimensions={0}, use_global_device_ids=true | all-gather | bytes 4608 | tf_op jit(solution)/shard_map/all_gather | solution.py:140
  230.0 175.5 %all-gather.26.cloned.1.call-done = f32[4096,2048]{1,0:T(8,128)} async-done(((f32[1024,2048]{1,0:T(8,128)}), f32[4096,2048]{1,0:T(8,128)}) %all-gather.26.cloned.1.call-update) | async-done | bytes 33554448 | tf_op jit(solution)/shard_map/all_gather | solution.py:15
  405.5 26.9 %reduce_sum.169 = f32[1024,2048]{1,0:T(8,128)} reduce(f32[4,1024,2048]{2,1,0:T(8,128)} %bitcast.223, f32[]{:T(128)} %constant.54.clone.1), dimensions={0}, to_apply=%region_9.10 | reduce | flops 6291456 | bytes 41943044 | tf_op jit(solution)/shard_map/reduce_sum | solution.py:15
  432.4 5.8 multiply_reduce_fusion.1
  444.2 63.0 %all-gather.20.cloned.1.call-done = bf16[2048,1536]{1,0:T(8,128)(2,1)} async-done(((bf16[256,1536]{1,0:T(8,128)(2,1)}), bf16[2048,1536]{1,0:T(8,128)(2,1)}) %all-gather.20.cloned.1.call-update) | async-done | bytes 6291472 | tf_op jit(solution)/shard_map/all_gather | solution.py:141
  507.2 11.7 fusion.78
  518.8 88.3 %all-gather.22.cloned.1.call-done = bf16[2048,1536]{1,0:T(8,128)(2,1)} async-done(((bf16[256,1536]{1,0:T(8,128)(2,1)}), bf16[2048,1536]{1,0:T(8,128)(2,1)}) %all-gather.22.cloned.1.call-update) | async-done | bytes 6291472 | tf_op jit(solution)/shard_map/all_gather | solution.py:142
  607.2 11.8 fusion.79
  619.0 89.0 %all-gather.24.cloned.1.call-done = bf16[1536,2048]{1,0:T(8,128)(2,1)} async-done(((bf16[1536,256]{1,0:T(8,128)(2,1)}), bf16[1536,2048]{1,0:T(8,128)(2,1)}) %all-gather.24.cloned.1.call-update) | async-done | bytes 6291472 | tf_op jit(solution)/shard_map/all_gather | solution.py:143
  708.0 16.4 multiply_convert_fusion.2
  724.4 10.0 fusion.80
  734.4 10.3 add_convert_fusion.1
  744.8 11.3 convolution_convert_fusion.3
  756.1 72.4 %all-reduce.13.cloned.1.call-done = bf16[1024,2048]{1,0:T(8,128)(2,1)} async-done(((bf16[1024,2048]{1,0:T(8,128)(2,1)}), bf16[1024,2048]{1,0:T(8,128)(2,1)}) %all-reduce.13.cloned.1.call-update) | async-done | bytes 4194320 | tf_op jit(solution)/shard_map/psum | solution.py:224
  828.5 6.0 fusion.5
  835.6 5.0 fusion.4
  848.7 5.1 fusion.7
  853.8 5.1 fusion.9
  877.4 4.9 convolution_convert_fusion.6
  882.5 5.1 fusion.33
  892.0 3.4 add_convert_fusion
  895.4 4.9 convolution_convert_fusion.7
  900.4 6.5 convolution_convert_fusion.5
  907.2 7.1 convolution_convert_fusion.4
  914.4 11.5 convolution_convert_fusion.2
  927.8 11.1 convolution_convert_fusion.1
  940.8 10.9 convolution_convert_fusion
  954.7 146.2 %all-reduce.15.cloned.1.call-done = (bf16[1024,2048]{1,0:T(8,128)(2,1)}, bf16[1024,2048]{1,0:T(8,128)(2,1)}) async-done(((bf16[1024,2048]{1,0:T(8,128)(2,1)}, bf16[1024,2048]{1,0:T(8,128)(2,1)}), (bf16[1024,2048]{1,0:T(8,128)(2,1)}, bf16[1024,2048]{1,0:T(8,128)(2,1)})) %all-reduce.15.cloned.1.call-update) | async-done | bytes 8388624 | tf_op jit(solution)/shard_map/psum | solution.py:209
  1100.9 6.5 multiply_reduce_fusion
  1107.5 22.0 %all-reduce.6 = (bf16[2048]{0:T(1024)(128)(2,1)S(1)}, bf16[128]{0:T(256)(128)(2,1)S(1)}, bf16[128]{0:T(256)(128)(2,1)S(1)}, bf16[2048]{0:T(1024)(128)(2,1)S(1)}) all-reduce(bf16[2048]{0:T(1024)(128)(2,1)S(1)} %get-tuple-element.84, bf16[128]{0:T(256)(128)(2,1)S(1)} %reduce_sum.180, ...), channel_id=3, replica_groups=mesh['dp'=8,'mp'=4] {'dp'}, use_global_device_ids=true, to_apply=%region_21.22.clone | all-reduce | flops 4352 | bytes 17408
  1129.7 38.8 %reduce-scatter.10.cloned.1.call-done = bf16[256,256]{1,0:T(8,128)(2,1)} async-done(((bf16[2048,256]{1,0:T(8,128)(2,1)}), bf16[256,256]{1,0:T(8,128)(2,1)}) %reduce-scatter.10.cloned.1.call-update) | async-done | bytes 131088 | tf_op jit(solution)/shard_map/reduce_scatter | solution.py:323
  1170.1 5.6 all-reduce.8
  1175.7 6.5 convert_element_type.272
  1183.3 56.7 %reduce-scatter.8.cloned.1.call-done = bf16[256,512]{1,0:T(8,128)(2,1)} async-done(((bf16[2048,512]{1,0:T(8,128)(2,1)}), bf16[256,512]{1,0:T(8,128)(2,1)}) %reduce-scatter.8.cloned.1.call-update) | async-done | bytes 262160 | tf_op jit(solution)/shard_map/reduce_scatter | solution.py:320
  1241.8 69.3 %reduce-scatter.14.cloned.1.call-done = bf16[512,256]{1,0:T(8,128)(2,1)} async-done(((bf16[512,2048]{1,0:T(8,128)(2,1)}), bf16[512,256]{1,0:T(8,128)(2,1)}) %reduce-scatter.14.cloned.1.call-update) | async-done | bytes 262160 | tf_op jit(solution)/shard_map/reduce_scatter | solution.py:329
  1316.1 6.0 multiply_add_fusion
  1322.1 109.9 %reduce-scatter.16.cloned.1.call-done = bf16[256,1536]{1,0:T(8,128)(2,1)} async-done(((bf16[2048,1536]{1,0:T(8,128)(2,1)}), bf16[256,1536]{1,0:T(8,128)(2,1)}) %reduce-scatter.16.cloned.1.call-update) | async-done | bytes 786448 | tf_op jit(solution)/shard_map/reduce_scatter | solution.py:337
  1434.4 118.5 %reduce-scatter.18.cloned.1.call-done = bf16[256,1536]{1,0:T(8,128)(2,1)} async-done(((bf16[2048,1536]{1,0:T(8,128)(2,1)}), bf16[256,1536]{1,0:T(8,128)(2,1)}) %reduce-scatter.18.cloned.1.call-update) | async-done | bytes 786448 | tf_op jit(solution)/shard_map/reduce_scatter | solution.py:340
  1555.4 119.0 %reduce-scatter.20.cloned.1.call-done = bf16[1536,256]{1,0:T(8,128)(2,1)} async-done(((bf16[1536,2048]{1,0:T(8,128)(2,1)}), bf16[1536,256]{1,0:T(8,128)(2,1)}) %reduce-scatter.20.cloned.1.call-update) | async-done | bytes 786448 | tf_op jit(solution)/shard_map/reduce_scatter | solution.py:343
  (262 shorter events, 97.0 us)
Async XLA Ops:
  7.2 34.9 %copy-start.47 = (u32[32]{0:T(128)S(1)}, u32[32]{0:T(128)}, u32[]{:S(2)}) copy-start(u32[32]{0:T(128)} %constant.106) | copy-start | bytes 388
  7.2 34.8 %copy-start.52 = (f32[16]{0:T(128)S(1)}, f32[16]{0:T(128)}, u32[]{:S(2)}) copy-start(f32[16]{0:T(128)} %param.19) | copy-start | bytes 196
  7.2 34.8 %copy-start.53 = (f32[16]{0:T(128)S(1)}, f32[16]{0:T(128)}, u32[]{:S(2)}) copy-start(f32[16]{0:T(128)} %param.18) | copy-start | bytes 196
  7.2 56.5 %all-gather.14.cloned.1.call-start = ((), (), s32[]{:S(2)}) async-start(), calls=%async_computation.8 | async-start | bytes 1179648 | tf_op jit(solution)/shard_map/all_gather | solution.py:126
  8.9 86.6 %all-gather.12.cloned.1.call-start = ((), (), s32[]{:S(2)}) async-start(), calls=%async_computation.7 | async-start | bytes 1179648 | tf_op jit(solution)/shard_map/all_gather | solution.py:127
  10.6 52.4 %copy-start.39 = (s32[1,1024]{1,0:T(1,128)S(1)}, s32[1,1024]{1,0:T(1,128)}, u32[]{:S(2)}) copy-start(s32[1,1024]{1,0:T(1,128)} %param.15) | copy-start | bytes 12292
  10.6 135.7 %all-gather.16.cloned.1.call-start = ((), (), s32[]{:S(2)}) async-start(), calls=%async_computation.9 | async-start | bytes 2359296 | tf_op jit(solution)/shard_map/all_gather | solution.py:125
  12.5 185.9 %all-gather.18.cloned.1.call-start = ((), (), s32[]{:S(2)}) async-start(), calls=%async_computation.10 | async-start | bytes 2359296 | tf_op jit(solution)/shard_map/all_gather | solution.py:128
  14.3 391.2 %all-gather.26.cloned.1.call-start = ((), (), s32[]{:S(2)}) async-start(), calls=%async_computation.22 | async-start | bytes 41943040 | tf_op jit(solution)/shard_map/all_gather | solution.py:15
  38.9 107.4 %copy-start.37 = (f32[8,1,256]{2,1,0:T(1,128)}, f32[8,1,256]{2,1,0:T(1,128)S(1)}, u32[]{:S(2)}) copy-start(f32[8,1,256]{2,1,0:T(1,128)S(1)} %convert_element_type.295) | copy-start | bytes 24580
  42.0 104.3 %copy-start.40 = (f32[1024]{0:T(1024)}, f32[1024]{0:T(1024)S(1)}, u32[]{:S(2)}) copy-start(f32[1024]{0:T(1024)S(1)} %add_rsqrt_fusion.3) | copy-start | bytes 12292
  61.0 7.1 copy-start.45
  62.9 89.5 %copy-start.7 = (f32[1024,128]{0,1:T(8,128)}, f32[1024,128]{0,1:T(8,128)S(1)}, u32[]{:S(2)}) copy-start(f32[1024,128]{0,1:T(8,128)S(1)} %pad_maximum_fusion.4) | copy-start | bytes 1572868
  62.9 89.4 %copy-start.9 = (f32[1024,128]{0,1:T(8,128)}, f32[1024,128]{0,1:T(8,128)S(1)}, u32[]{:S(2)}) copy-start(f32[1024,128]{0,1:T(8,128)S(1)} %pad_maximum_fusion.5) | copy-start | bytes 1572868
  62.9 166.5 %copy-start.42 = (f32[128]{0:T(128)}, f32[128]{0:T(128)S(1)}, u32[]{:S(2)}) copy-start(f32[128]{0:T(128)S(1)} %convert_element_type.238) | copy-start | bytes 1540
  69.1 88.0 %copy-start.16 = (bf16[1024,2,128,1]{0,2,3,1:T(8,128)(2,1)}, bf16[1024,2,128,1]{0,2,3,1:T(8,128)(2,1)S(1)}, u32[]{:S(2)}) copy-start(bf16[1024,2,128,1]{0,2,3,1:T(8,128)(2,1)S(1)} %fusion.64) | copy-start | bytes 1572868
  155.6 4.4 copy-start
  163.9 41.7 %copy-start.33 = (bf16[1024,2,2,128]{0,3,2,1:T(8,128)(2,1)}, bf16[1024,2,2,128]{0,3,2,1:T(8,128)(2,1)S(1)}, u32[]{:S(2)}) copy-start(bf16[1024,2,2,128]{0,3,2,1:T(8,128)(2,1)S(1)} %pad_maximum_fusion.3) | copy-start | bytes 3145732
  205.6 6.0 copy-start.51
  205.7 301.5 %all-gather.20.cloned.1.call-start = ((), (), s32[]{:S(2)}) async-start(), calls=%async_computation.11 | async-start | bytes 7077888 | tf_op jit(solution)/shard_map/all_gather | solution.py:141
  208.0 399.2 %all-gather.22.cloned.1.call-start = ((), (), s32[]{:S(2)}) async-start(), calls=%async_computation.12 | async-start | bytes 7077888 | tf_op jit(solution)/shard_map/all_gather | solution.py:142
  210.6 497.4 %all-gather.24.cloned.1.call-start = ((), (), s32[]{:S(2)}) async-start(), calls=%async_computation.13 | async-start | bytes 7077888 | tf_op jit(solution)/shard_map/all_gather | solution.py:143
  211.6 616.9 %all-reduce.13.cloned.1.call-start = ((), (), s32[]{:S(2)}) async-start(), calls=%async_computation.14 | async-start | bytes 8388608 | tf_op jit(solution)/shard_map/psum | solution.py:224
  438.2 3.3 copy-start.2
  724.4 10.0 copy-start.54
  724.4 10.0 copy-start.48
  744.7 208.4 %reduce-scatter.12.cloned.1.call-start = ((), (), s32[]{:S(2)}) async-start(), calls=%async_computation.17 | async-start | bytes 1179648 | tf_op jit(solution)/shard_map/reduce_scatter | solution.py:326
  828.5 6.0 copy-start.12
  828.5 7.1 copy-start.24
  828.5 15.4 slice-start
  835.6 5.0 copy-start.50
  835.6 8.4 slice-start.1
  844.0 4.4 slice-start.2
  853.8 5.1 copy-start.21
  862.6 12.5 copy-start.13
  868.9 6.2 copy-start.14
  877.3 5.2 copy-start.44
  882.3 218.7 %all-reduce.15.cloned.1.call-start = ((), (), s32[]{:S(2)}) async-start(), calls=%async_computation.23 | async-start | bytes 16777216 | tf_op jit(solution)/shard_map/psum | solution.py:209
  882.5 5.1 copy-start.22
  882.5 5.4 copy-start.29
  895.4 5.0 copy-start.32
  895.4 273.1 %reduce-scatter.10.cloned.1.call-start = ((), (), s32[]{:S(2)}) async-start(), calls=%async_computation.16 | async-start | bytes 1179648 | tf_op jit(solution)/shard_map/reduce_scatter | solution.py:323
  900.3 6.9 copy-start.34
  900.4 339.6 %reduce-scatter.8.cloned.1.call-start = ((), (), s32[]{:S(2)}) async-start(), calls=%async_computation.15 | async-start | bytes 2359296 | tf_op jit(solution)/shard_map/reduce_scatter | solution.py:320
  907.0 404.2 %reduce-scatter.14.cloned.1.call-start = ((), (), s32[]{:S(2)}) async-start(), calls=%async_computation.18 | async-start | bytes 2359296 | tf_op jit(solution)/shard_map/reduce_scatter | solution.py:329
  914.4 517.6 %reduce-scatter.16.cloned.1.call-start = ((), (), s32[]{:S(2)}) async-start(), calls=%async_computation.19 | async-start | bytes 7077888 | tf_op jit(solution)/shard_map/reduce_scatter | solution.py:337
  925.9 627.0 %reduce-scatter.18.cloned.1.call-start = ((), (), s32[]{:S(2)}) async-start(), calls=%async_computation.20 | async-start | bytes 7077888 | tf_op jit(solution)/shard_map/reduce_scatter | solution.py:340
  938.9 735.5 %reduce-scatter.20.cloned.1.call-start = ((), (), s32[]{:S(2)}) async-start(), calls=%async_computation.21 | async-start | bytes 7077888 | tf_op jit(solution)/shard_map/reduce_scatter | solution.py:343
  (30 other events, 58.3 us)
Sparse Core Ops, SparseCore 0:
  10.7 42.9 all-gather.13
  56.4 39.0 all-gather.11
  98.2 48.0 all-gather.15
  148.8 49.5 all-gather.17
  205.8 199.6 all-gather.25
  408.1 99.0 all-gather.19
  509.9 97.1 all-gather.21
  609.8 98.1 all-gather.23
  744.8 83.6 all-reduce.12
  882.4 63.6 reduce-scatter.11
  948.7 152.2 all-reduce.14
  1104.8 63.6 reduce-scatter.9
  1173.0 66.9 reduce-scatter.7
  1243.8 67.2 reduce-scatter.13
  1315.0 116.9 reduce-scatter.15
  1435.8 117.0 reduce-scatter.17
  1556.8 117.5 reduce-scatter.19
